TPU v7x, 32 devices: a whole 2x2x4 slice. The times are simulated.
32 devices in a mesh: seg: 4 (over y, core), dp: 8 (over z, x).
Axes of the slice: x: 2, y: 2, z: 4, core: 2. Of those that a mesh axis runs over, the one named last changes fastest.
Arguments:
- queries: bfloat16 [8, 512, 2048], P('dp', 'seg'), may hold values from -32 to 32
- keys: bfloat16 [8, 512, 2048], P('dp', 'seg'), may hold values from -6 to 6
- values: bfloat16 [8, 512, 2048], P('dp', 'seg'), may hold values from -6 to 6
- rel_keys: bfloat16 [256, 2048], replicated, may hold values from -6 to 6
- bias_u: float32 [2048], replicated, may hold values from -3 to 3
- bias_v: float32 [2048], replicated, may hold values from -3 to 3
- d_out: bfloat16 [8, 512, 2048], P('dp', 'seg'), may hold values from -6 to 6
Outputs:
- d_queries: bfloat16 [8, 512, 2048], P('dp', 'seg')
- d_keys: bfloat16 [8, 512, 2048], P('dp', 'seg')
- d_rel_keys: float32 [256, 2048], P('seg', 'dp')
- d_bias_u: float32 [2048], replicated
- d_bias_v: float32 [2048], replicated
All inputs are finite; a program needn't handle non-finite values.
Results may differ from a plain program's by a relative error of at most 0.0068.
Values may be sent and summed in bfloat16 or wider, within the bound.
No kernel may reach another device: no remote copies, remote signals or barrier semaphores. Data moves between devices by JAX's collectives and lax.ppermute only.
A program may use at most 64 MiB of HBM per device.

v0:
```python
import jax
import jax.numpy as jnp
from jax import lax
from jax.sharding import PartitionSpec as P

DH = 128


def from_behind(block, axis, distance):
    devices = range(lax.axis_size(axis))
    route = [(i - distance, i) for i in devices if i - distance in devices]
    return lax.ppermute(block, axis, route)


def product(form, left, right):
    return jnp.einsum(form, left, right, preferred_element_type=jnp.float32)


def shift_rel(raw_scores):
    head_count, seg_rows, key_count = raw_scores.shape
    padded = jnp.pad(raw_scores, ((0, 0), (0, 0), (1, 0)))
    folded = padded.reshape(head_count, key_count + 1, seg_rows)[:, 1:, :]
    return folded.reshape(head_count, seg_rows, key_count)


def local_grads(
    query_rows,
    key_local,
    value_local,
    key_memory,
    value_memory,
    rel_keys,
    bias_u,
    bias_v,
    d_out,
    mem_on,
):
    seg_rows = query_rows.shape[0]
    mem_len = key_memory.shape[0]
    key_count = seg_rows + mem_len
    head_count = query_rows.shape[1] // DH
    keys_all = jnp.concatenate([key_memory, key_local], 0).reshape(key_count, head_count, DH)
    values_all = jnp.concatenate([value_memory, value_local], 0).reshape(key_count, head_count, DH)
    rel_heads = rel_keys.reshape(key_count, head_count, DH)
    query_wide = query_rows.astype(jnp.float32)
    q_content = (query_wide + bias_u).astype(jnp.bfloat16).reshape(seg_rows, head_count, DH)
    q_position = (query_wide + bias_v).astype(jnp.bfloat16).reshape(seg_rows, head_count, DH)
    content = product("ihd,jhd->hij", q_content, keys_all)
    position = shift_rel(product("ihd,phd->hip", q_position, rel_heads))
    score_scale = DH ** (-0.5)
    row_index = jnp.arange(seg_rows, dtype=jnp.int32)[:, None]
    key_index = jnp.arange(key_count, dtype=jnp.int32)[None, :]
    allowed = (key_index <= row_index + mem_len) & ((key_index >= mem_len) | mem_on)
    scores = jnp.where(allowed[None], score_scale * (content + position), -1e30)
    row_max = jnp.max(scores, axis=-1, keepdims=True)
    raised = jnp.exp(scores - row_max)
    weights = raised / jnp.sum(raised, axis=-1, keepdims=True)
    d_heads = d_out.reshape(seg_rows, head_count, DH)
    d_weights = product("ihd,jhd->hij", d_heads, values_all)
    centred = d_weights - jnp.sum(weights * d_weights, axis=-1, keepdims=True)
    grad_scores = (score_scale * weights * centred).astype(jnp.bfloat16)
    d_content = product("hij,jhd->ihd", grad_scores, keys_all)
    d_keys = product("hij,ihd->jhd", grad_scores[:, :, mem_len:], q_content)
    zero_raw = jnp.zeros((head_count, seg_rows, key_count), jnp.bfloat16)
    unshift = jax.vjp(shift_rel, zero_raw)[1]
    grad_rel = unshift(grad_scores)[0]
    d_position = product("hip,phd->ihd", grad_rel, rel_heads)
    d_rel = product("hip,ihd->phd", grad_rel, q_position).reshape(key_count, head_count * DH)
    d_query = (d_content + d_position).reshape(seg_rows, head_count * DH).astype(jnp.bfloat16)
    d_key = d_keys.reshape(seg_rows, head_count * DH).astype(jnp.bfloat16)
    return (
        d_query,
        d_key,
        d_rel,
        jnp.sum(d_content, 0).reshape(-1),
        jnp.sum(d_position, 0).reshape(-1),
    )


def shards(queries, keys, values, rel_keys, bias_u, bias_v, d_out):
    seg_rows = queries.shape[1]
    mem_len = rel_keys.shape[0] - seg_rows
    memory = from_behind((keys[0, seg_rows - mem_len :], values[0, seg_rows - mem_len :]), "seg", 1)
    mem_on = lax.axis_index("seg") > 0
    d_query, d_key, d_rel, d_content, d_position = local_grads(
        queries[0],
        keys[0],
        values[0],
        memory[0],
        memory[1],
        rel_keys,
        bias_u,
        bias_v,
        d_out[0],
        mem_on,
    )
    bias_grads = lax.psum((d_content, d_position), ("seg", "dp"))
    shared = lax.psum_scatter(d_rel, "seg", scatter_dimension=0, tiled=True)
    shared = lax.psum_scatter(shared, "dp", scatter_dimension=1, tiled=True)
    return (d_query[None], d_key[None], shared, bias_grads[0], bias_grads[1])


def solution(mesh):
    placed = (
        P("dp", "seg", None),
        P("dp", "seg", None),
        P("dp", "seg", None),
        P(),
        P(),
        P(),
        P("dp", "seg", None),
    )
    return jax.shard_map(
        shards,
        mesh=mesh,
        in_specs=placed,
        out_specs=(P("dp", "seg", None), P("dp", "seg", None), P("seg", "dp"), P(), P()),
        check_vma=False,
    )
```

profile of v0, /device:TPU:0, one launch (start us, length us, event | category | flops | bytes accessed | tf_op | source)
XLA Modules:
  0.0 174.5 jit_solution(12217957348637252360)
XLA Ops:
  7.2 0.0 copy-start.2
  7.2 0.0 copy-start.1
  7.2 0.0 reduce-scatter.3.cloned.1.call-start
  7.2 2.1 %copy.33 = bf16[1,128,2048]{1,2,0:T(8,128)(2,1)} copy(bf16[1,128,2048]{2,1,0:T(8,128)(2,1)} %param.9) | data formatting | bytes 1048576 | tf_op args[2]
  9.4 3.2 %collective-permute-start.1 = (bf16[128,2048]{0,1:T(8,128)(2,1)}, bf16[128,2048]{0,1:T(8,128)(2,1)}, u32[]{:S(2)}, u32[]{:S(2)}) collective-permute-start(bf16[128,2048]{0,1:T(8,128)(2,1)} %bitcast.5), channel_id=1, source_target_pairs={{0,8},{8,16},{16,24},{1,9},{9,17},{17,25},{2,10},{10,18},{18,26},{... | collective-permute-start | bytes 1572872 | tf_op jit(solution)/shard_map/ppermute | solution.py:12
  12.5 2.0 %copy.24 = bf16[1,128,2048]{1,2,0:T(8,128)(2,1)} copy(bf16[1,128,2048]{2,1,0:T(8,128)(2,1)} %param.8) | data formatting | bytes 1048576 | tf_op args[1]
  14.6 0.0 copy-start.3
  14.6 4.7 %collective-permute-start = (bf16[128,2048]{0,1:T(8,128)(2,1)}, bf16[128,2048]{0,1:T(8,128)(2,1)}, u32[]{:S(2)}, u32[]{:S(2)}) collective-permute-start(bf16[128,2048]{0,1:T(8,128)(2,1)} %bitcast), channel_id=1, source_target_pairs={{0,8},{8,16},{16,24},{1,9},{9,17},{17,25},{2,10},{10,18},{18,26},{... | collective-permute-start | bytes 1572872 | tf_op jit(solution)/shard_map/ppermute | solution.py:12
  19.3 0.0 copy-done.2
  19.3 0.2 copy.48
  19.5 0.0 copy-done.1
  19.5 0.5 copy.49
  20.0 0.0 copy-done.3
  20.0 0.8 fusion.15
  20.9 2.6 %pad.12 = f32[16,128,257]{2,1,0:T(8,128)} pad(f32[16,128,256]{2,1,0:T(8,128)S(1)} %fusion.15, f32[]{:T(128)} %constant.4.clone.1), padding=0_0x0_0x1_0 | pad | bytes 4202500 | tf_op jit(solution)/shard_map/jit(_pad)/pad | solution.py:21
  23.4 4.7 %reshape.134 = f32[16,257,128]{2,1,0:T(8,128)} reshape(f32[16,128,257]{2,1,0:T(8,128)} %pad.12) | data formatting | bytes 4210688 | tf_op jit(solution)/shard_map/reshape | solution.py:22
  28.1 3.2 %slice.9 = f32[16,256,128]{2,1,0:T(8,128)} slice(f32[16,257,128]{2,1,0:T(8,128)} %reshape.134), slice={[0:16], [1:257], [0:128]} | slice | bytes 4194304 | tf_op jit(solution)/shard_map/slice | solution.py:22
  31.3 2.9 %reshape.135 = f32[16,128,256]{2,1,0:T(8,128)} reshape(f32[16,256,128]{2,1,0:T(8,128)} %slice.9) | data formatting | bytes 4194304 | tf_op jit(solution)/shard_map/reshape | solution.py:23
  34.2 1.3 copy.36
  35.5 1.1 copy.50
  36.6 2.0 %copy.27 = bf16[128,16,128]{2,0,1:T(8,128)(2,1)} copy(bf16[128,16,128]{0,2,1:T(8,128)(2,1)} %bitcast.2) | data formatting | bytes 1048576 | tf_op jit(solution)/shard_map/concatenate | solution.py:42
  38.7 0.1 fusion.16
  38.8 0.0 collective-permute-done.1
  38.8 2.0 %copy.35 = bf16[128,16,128]{2,0,1:T(8,128)(2,1)} copy(bf16[128,16,128]{0,2,1:T(8,128)(2,1)} %bitcast.6) | data formatting | bytes 1048576 | tf_op jit(solution)/shard_map/concatenate | solution.py:43
  40.8 0.0 collective-permute-done
  40.9 2.0 %copy.26 = bf16[128,16,128]{2,0,1:T(8,128)(2,1)} copy(bf16[128,16,128]{0,2,1:T(8,128)(2,1)} %bitcast.1) | data formatting | bytes 1048576 | tf_op jit(solution)/shard_map/concatenate | solution.py:42
  42.9 2.8 %fusion.6 = f32[16,256,128]{1,2,0:T(8,128)} fusion(bf16[128,16,128]{2,0,1:T(8,128)(2,1)S(1)} %copy.36, bf16[128,16,128]{2,0,1:T(8,128)(2,1)} %copy.35, bf16[128,16,128]{2,1,0:T(8,128)(2,1)S(1)} %bitcast.45), kind=kOutput, calls=%fused_computation.14 | convolution fusion | flops 136314880 | bytes 3670016 | tf_op jit(solution)/shard_map/ihd,jhd->hij/dot_general | solution.py:16
  45.7 0.0 copy-done.4
  45.7 5.4 %fusion.2 = (f32[16,128]{1,0:T(8,128)S(1)}, f32[16,128,256]{2,1,0:T(8,128)}) fusion(f32[16,256,128]{1,2,0:T(8,128)} %fusion.6, f32[16,128,256]{2,1,0:T(8,128)} %reshape.135, pred[128,256]{1,0:T(8,128)(4,1)S(1)} %fusion.16, bf16[128,16,128]{2,0,1:T(8,128)(2,1)} %copy.27, bf16[128,16,128]{2,0,1:T(8,128)(2,1)} %copy.26, f32[128,16,128]{0,2,1:T(8,128)S(1)} %bitcast.39, ...), kind=kOutput, calls=%fused_computation.4 | convolution fusion | flops 140511744 | bytes 8437760 | tf_op jit(solution)/shard_map/div | solution.py:57
  51.2 2.6 %fusion.4 = bf16[16,128,256]{2,1,0:T(8,128)(2,1)S(1)} fusion(f32[16,256,128]{1,2,0:T(8,128)} %fusion.6, f32[16,128,256]{2,1,0:T(8,128)} %get-tuple-element.21, f32[16,128]{1,0:T(8,128)S(1)} %get-tuple-element.20), kind=kLoop, calls=%fused_computation.6 | loop fusion | flops 2097152 | bytes 5251072 | tf_op jit(solution)/shard_map/convert_element_type | solution.py:61
  53.7 1.2 reshape.136
  54.9 2.5 %pad.13 = bf16[16,257,128]{2,1,0:T(8,128)(2,1)} pad(bf16[16,256,128]{2,1,0:T(8,128)(2,1)} %reshape.136, bf16[]{:T(256)} %constant.22.clone.1), padding=0_0x1_0x0_0 | pad | bytes 2101250 | tf_op jit(solution)/shard_map/transpose(jvp())/pad | solution.py:22
  57.4 5.0 %reshape.137 = bf16[16,128,257]{2,1,0:T(8,128)(2,1)} reshape(bf16[16,257,128]{2,1,0:T(8,128)(2,1)} %pad.13) | data formatting | bytes 2105344 | tf_op jit(solution)/shard_map/transpose(jvp())/reshape | solution.py:22
  62.5 3.6 %fusion.10 = f32[16,128,256]{2,1,0:T(8,128)} fusion(bf16[16,128,257]{2,1,0:T(8,128)(2,1)} %reshape.137, f32[128,16,128]{0,2,1:T(8,128)S(1)} %bitcast.40, f32[16,128]{1,0:T(8,128)S(1)} %bitcast.50), kind=kOutput, calls=%fused_computation.21 | convolution fusion | flops 134742016 | bytes 4202496 | tf_op jit(solution)/shard_map/hip,ihd->phd/dot_general | solution.py:16
  66.1 2.9 %copy.41 = f32[256,2048]{1,0:T(8,128)} copy(f32[256,2048]{0,1:T(8,128)} %bitcast.44) | data formatting | bytes 4194304 | tf_op jit(solution)/shard_map/reshape | solution.py:68
  68.9 0.0 reduce-scatter.3.cloned.1.call-update
  69.0 0.2 reduce-scatter.5.cloned.1.call-start
  69.2 31.7 %reduce-scatter.3.cloned.1.call-done = f32[64,2048]{1,0:T(8,128)} async-done(((f32[256,2048]{1,0:T(8,128)}), f32[64,2048]{1,0:T(8,128)}) %reduce-scatter.3.cloned.1.call-update) | async-done | bytes 524304 | tf_op jit(solution)/shard_map/reduce_scatter | solution.py:98
  100.8 0.0 reduce-scatter.5.cloned.1.call-update
  100.9 0.0 copy-start
  100.9 1.8 %convolution_bitcast_fusion.1 = f32[128,16,128]{0,2,1:T(8,128)S(1)} fusion(bf16[16,128,256]{2,1,0:T(8,128)(2,1)S(1)} %fusion.4, bf16[128,16,128]{2,0,1:T(8,128)(2,1)} %copy.27, bf16[128,16,128]{2,0,1:T(8,128)(2,1)} %copy.26), kind=kOutput, calls=%fused_computation.11 | convolution fusion | flops 136314880 | bytes 3145728 | tf_op jit(solution)/shard_map/hij,jhd->ihd/dot_general | solution.py:16
  102.7 0.0 copy-done
  102.7 1.4 fusion.21
  104.0 2.0 %copy.42 = bf16[1,128,2048]{2,1,0:T(8,128)(2,1)} copy(bf16[1,128,2048]{1,2,0:T(8,128)(2,1)} %bitcast.46) | data formatting | bytes 1048576
  106.1 0.5 convolution_convert_fusion
  106.5 1.0 copy.43
  107.6 39.6 %all-reduce.2 = (f32[2048]{0:T(1024)}, f32[2048]{0:T(1024)}) all-reduce(f32[2048]{0:T(1024)S(1)} %bitcast.52, f32[2048]{0:T(1024)S(1)} %bitcast.51), channel_id=1, replica_groups=mesh['seg'=4,'dp'=8] {'seg','dp'}, use_global_device_ids=true, to_apply=%region_6.7 | all-reduce | flops 4096 | bytes 32768 | tf_op jit(solution)/shard_map/psum | solution.py:97
  147.2 20.5 %reduce-scatter.5.cloned.1.call-done = f32[64,256]{1,0:T(8,128)} async-done(((f32[64,2048]{1,0:T(8,128)}), f32[64,256]{1,0:T(8,128)}) %reduce-scatter.5.cloned.1.call-update) | async-done | bytes 65552 | tf_op jit(solution)/shard_map/reduce_scatter | solution.py:99
  (3 shorter events, 0.0 us)
Async XLA Ops:
  7.2 12.1 %copy-start.2 = (bf16[1,128,2048]{2,1,0:T(8,128)(2,1)S(1)}, bf16[1,128,2048]{2,1,0:T(8,128)(2,1)}, u32[]{:S(2)}) copy-start(bf16[1,128,2048]{2,1,0:T(8,128)(2,1)} %param.7) | copy-start | bytes 1572868
  7.2 12.3 %copy-start.1 = (bf16[256,2048]{1,0:T(8,128)(2,1)S(1)}, bf16[256,2048]{1,0:T(8,128)(2,1)}, u32[]{:S(2)}) copy-start(bf16[256,2048]{1,0:T(8,128)(2,1)} %param.10) | copy-start | bytes 3145732
  7.2 93.7 %reduce-scatter.3.cloned.1.call-start = ((), (), s32[]{:S(2)}) async-start(), calls=%async_computation.2 | async-start | bytes 2621440 | tf_op jit(solution)/shard_map/reduce_scatter | solution.py:98
  9.4 29.4 %collective-permute-start.1 = (bf16[128,2048]{0,1:T(8,128)(2,1)}, bf16[128,2048]{0,1:T(8,128)(2,1)}, u32[]{:S(2)}, u32[]{:S(2)}) collective-permute-start(bf16[128,2048]{0,1:T(8,128)(2,1)} %bitcast.5), channel_id=1, source_target_pairs={{0,8},{8,16},{16,24},{1,9},{9,17},{17,25},{2,10},{10,18},{18,26},{... | collective-permute-start | bytes 1572872 | tf_op jit(solution)/shard_map/ppermute | solution.py:12
  14.6 5.4 %copy-start.3 = (f32[2048]{0:T(1024)S(1)}, f32[2048]{0:T(1024)}, u32[]{:S(2)}) copy-start(f32[2048]{0:T(1024)} %param.12) | copy-start | bytes 24580
  14.6 26.3 %collective-permute-start = (bf16[128,2048]{0,1:T(8,128)(2,1)}, bf16[128,2048]{0,1:T(8,128)(2,1)}, u32[]{:S(2)}, u32[]{:S(2)}) collective-permute-start(bf16[128,2048]{0,1:T(8,128)(2,1)} %bitcast), channel_id=1, source_target_pairs={{0,8},{8,16},{16,24},{1,9},{9,17},{17,25},{2,10},{10,18},{18,26},{... | collective-permute-start | bytes 1572872 | tf_op jit(solution)/shard_map/ppermute | solution.py:12
  42.9 2.8 %copy-start.4 = (f32[2048]{0:T(1024)S(1)}, f32[2048]{0:T(1024)}, u32[]{:S(2)}) copy-start(f32[2048]{0:T(1024)} %param.11) | copy-start | bytes 24580
  69.0 98.7 %reduce-scatter.5.cloned.1.call-start = ((), (), s32[]{:S(2)}) async-start(), calls=%async_computation.3 | async-start | bytes 589824 | tf_op jit(solution)/shard_map/reduce_scatter | solution.py:99
  100.9 1.8 %copy-start = (bf16[16,128,257]{2,1,0:T(8,128)(2,1)S(1)}, bf16[16,128,257]{2,1,0:T(8,128)(2,1)}, u32[]{:S(2)}) copy-start(bf16[16,128,257]{2,1,0:T(8,128)(2,1)} %reshape.137) | copy-start | bytes 3158020
Sparse Core Ops, SparseCore 0:
  69.1 31.7 reduce-scatter.2
  105.1 62.5 reduce-scatter.4
where the time goes:
time: 175 us
  waiting for transfers between devices  52.2 us (30%)
  local copies, waits for them, and re-layouts  41.5 us (24%)
  blocking collectives  39.6 us (23%)
  matrix products  16.3 us (9%)
  between operations  14.2 us (8%)
  starting transfers between devices  8.1 us (5%)
  other arithmetic  2.66 us (2%)
    psum x1, blocking collectives, shards(): bias_grads = lax.psum((d_content, d_position), ('seg', 'dp'))  39.6 us
    reduce_scatter x1, waiting for transfers between devices, shards(): shared = lax.psum_scatter(d_rel, 'seg', scatter_dimension=0, tiled=True)  31.7 us
    reduce_scatter x1, waiting for transfers between devices, shards(): shared = lax.psum_scatter(shared, 'dp', scatter_dimension=1, tiled=True)  20.5 us
    dot_general x6, matrix products, product(): return jnp.einsum(form, left, right, preferred_element_type=jnp.float32)  10.9 us
    reshape x2, local copies, waits for them, and re-layouts, shift_rel(): folded = padded.reshape(head_count, key_count + 1, seg_rows)[:, 1:, :]  9.72 us
    unnamed x15, local copies, waits for them, and re-layouts  8.4 us
    ppermute x2, starting transfers between devices, from_behind(): return lax.ppermute(block, axis, route)  7.84 us
    div x1, matrix products, local_grads(): weights = raised / jnp.sum(raised, axis=-1, keepdims=True)  5.43 us
  transfers between devices with their start and end apart: 4, of which 2 were waited for; matrix products, arithmetic and copies ran while one was open for 17% of the time, Pallas kernels for 0%

commit v1 on v0

--- a/solution.py
+++ b/solution.py
@@ -94,7 +94,9 @@
         d_out[0],
         mem_on,
     )
-    bias_grads = lax.psum((d_content, d_position), ("seg", "dp"))
+    bias_grads = (d_content, d_position)
+    for over in ("seg", "dp"):
+        bias_grads = lax.psum(bias_grads, over)
     shared = lax.psum_scatter(d_rel, "seg", scatter_dimension=0, tiled=True)
     shared = lax.psum_scatter(shared, "dp", scatter_dimension=1, tiled=True)
     return (d_query[None], d_key[None], shared, bias_grads[0], bias_grads[1])

time: 175 us -> 175 us (level)
  waiting for transfers between devices: 52.2 us -> 43.8 us
  blocking collectives: 39.6 us -> 47.9 us
    reduce_scatter x1, waiting for transfers between devices: 20.5 us -> 12.1 us  [shards(): shared = lax.psum_scatter(shared, 'dp', scatter_dimension=1, tiled=True)]
    psum x1 -> x2, blocking collectives: 39.6 us -> 47.9 us  [shards(): bias_grads = lax.psum(bias_grads, over)]
where the time goes in v1:
time: 175 us; the launch traced here: 174 us
  blocking collectives  47.9 us (27%)
  waiting for transfers between devices  43.8 us (25%)
  local copies, waits for them, and re-layouts  41.5 us (24%)
  matrix products  16.3 us (9%)
  between operations  14.2 us (8%)
  starting transfers between devices  8.1 us (5%)
  other arithmetic  2.66 us (2%)
    psum x2, blocking collectives, shards(): bias_grads = lax.psum(bias_grads, over)  47.9 us
    reduce_scatter x1, waiting for transfers between devices, shards(): shared = lax.psum_scatter(d_rel, 'seg', scatter_dimension=0, tiled=True)  31.7 us
    reduce_scatter x1, waiting for transfers between devices, shards(): shared = lax.psum_scatter(shared, 'dp', scatter_dimension=1, tiled=True)  12.1 us
    dot_general x6, matrix products, product(): return jnp.einsum(form, left, right, preferred_element_type=jnp.float32)  10.9 us
    reshape x2, local copies, waits for them, and re-layouts, shift_rel(): folded = padded.reshape(head_count, key_count + 1, seg_rows)[:, 1:, :]  9.72 us
    unnamed x15, local copies, waits for them, and re-layouts  8.4 us
    ppermute x2, starting transfers between devices, from_behind(): return lax.ppermute(block, axis, route)  7.84 us
    div x1, matrix products, local_grads(): weights = raised / jnp.sum(raised, axis=-1, keepdims=True)  5.43 us
  transfers between devices with their start and end apart: 4, of which 2 were waited for; matrix products, arithmetic and copies ran while one was open for 17% of the time, Pallas kernels for 0%

profile of v1, /device:TPU:0, one launch (start us, length us, event | category | flops | bytes accessed | tf_op | source)
XLA Modules:
  0.0 174.4 jit_solution(8944122766898694312)
XLA Ops:
  7.2 0.0 copy-start.2
  7.2 0.0 copy-start.1
  7.2 0.0 reduce-scatter.3.cloned.1.call-start
  7.2 2.1 %copy.33 = bf16[1,128,2048]{1,2,0:T(8,128)(2,1)} copy(bf16[1,128,2048]{2,1,0:T(8,128)(2,1)} %param.9) | data formatting | bytes 1048576 | tf_op args[2]
  9.4 3.2 %collective-permute-start.1 = (bf16[128,2048]{0,1:T(8,128)(2,1)}, bf16[128,2048]{0,1:T(8,128)(2,1)}, u32[]{:S(2)}, u32[]{:S(2)}) collective-permute-start(bf16[128,2048]{0,1:T(8,128)(2,1)} %bitcast.5), channel_id=1, source_target_pairs={{0,8},{8,16},{16,24},{1,9},{9,17},{17,25},{2,10},{10,18},{18,26},{... | collective-permute-start | bytes 1572872 | tf_op jit(solution)/shard_map/ppermute | solution.py:12
  12.5 2.0 %copy.24 = bf16[1,128,2048]{1,2,0:T(8,128)(2,1)} copy(bf16[1,128,2048]{2,1,0:T(8,128)(2,1)} %param.8) | data formatting | bytes 1048576 | tf_op args[1]
  14.6 4.7 %collective-permute-start = (bf16[128,2048]{0,1:T(8,128)(2,1)}, bf16[128,2048]{0,1:T(8,128)(2,1)}, u32[]{:S(2)}, u32[]{:S(2)}) collective-permute-start(bf16[128,2048]{0,1:T(8,128)(2,1)} %bitcast), channel_id=1, source_target_pairs={{0,8},{8,16},{16,24},{1,9},{9,17},{17,25},{2,10},{10,18},{18,26},{... | collective-permute-start | bytes 1572872 | tf_op jit(solution)/shard_map/ppermute | solution.py:12
  19.3 0.0 copy-done.2
  19.3 0.2 copy.48
  19.5 0.0 copy-done.1
  19.5 0.5 copy.49
  20.0 0.0 copy-done.3
  20.0 0.8 fusion.15
  20.9 2.6 %pad.12 = f32[16,128,257]{2,1,0:T(8,128)} pad(f32[16,128,256]{2,1,0:T(8,128)S(1)} %fusion.15, f32[]{:T(128)} %constant.4.clone.1), padding=0_0x0_0x1_0 | pad | bytes 4202500 | tf_op jit(solution)/shard_map/jit(_pad)/pad | solution.py:21
  23.4 4.7 %reshape.134 = f32[16,257,128]{2,1,0:T(8,128)} reshape(f32[16,128,257]{2,1,0:T(8,128)} %pad.12) | data formatting | bytes 4210688 | tf_op jit(solution)/shard_map/reshape | solution.py:22
  28.1 3.2 %slice.9 = f32[16,256,128]{2,1,0:T(8,128)} slice(f32[16,257,128]{2,1,0:T(8,128)} %reshape.134), slice={[0:16], [1:257], [0:128]} | slice | bytes 4194304 | tf_op jit(solution)/shard_map/slice | solution.py:22
  31.3 2.9 %reshape.135 = f32[16,128,256]{2,1,0:T(8,128)} reshape(f32[16,256,128]{2,1,0:T(8,128)} %slice.9) | data formatting | bytes 4194304 | tf_op jit(solution)/shard_map/reshape | solution.py:23
  34.2 1.3 copy.36
  35.5 1.1 copy.50
  36.6 2.0 %copy.27 = bf16[128,16,128]{2,0,1:T(8,128)(2,1)} copy(bf16[128,16,128]{0,2,1:T(8,128)(2,1)} %bitcast.2) | data formatting | bytes 1048576 | tf_op jit(solution)/shard_map/concatenate | solution.py:42
  38.7 0.1 fusion.16
  38.8 0.0 collective-permute-done.1
  38.8 2.0 %copy.35 = bf16[128,16,128]{2,0,1:T(8,128)(2,1)} copy(bf16[128,16,128]{0,2,1:T(8,128)(2,1)} %bitcast.6) | data formatting | bytes 1048576 | tf_op jit(solution)/shard_map/concatenate | solution.py:43
  40.8 0.0 collective-permute-done
  40.9 2.0 %copy.26 = bf16[128,16,128]{2,0,1:T(8,128)(2,1)} copy(bf16[128,16,128]{0,2,1:T(8,128)(2,1)} %bitcast.1) | data formatting | bytes 1048576 | tf_op jit(solution)/shard_map/concatenate | solution.py:42
  42.9 2.8 %fusion.6 = f32[16,256,128]{1,2,0:T(8,128)} fusion(bf16[128,16,128]{2,0,1:T(8,128)(2,1)S(1)} %copy.36, bf16[128,16,128]{2,0,1:T(8,128)(2,1)} %copy.35, bf16[128,16,128]{2,1,0:T(8,128)(2,1)S(1)} %bitcast.45), kind=kOutput, calls=%fused_computation.14 | convolution fusion | flops 136314880 | bytes 3670016 | tf_op jit(solution)/shard_map/ihd,jhd->hij/dot_general | solution.py:16
  45.7 0.0 copy-done.4
  45.7 5.4 %fusion.2 = (f32[16,128]{1,0:T(8,128)S(1)}, f32[16,128,256]{2,1,0:T(8,128)}) fusion(f32[16,256,128]{1,2,0:T(8,128)} %fusion.6, f32[16,128,256]{2,1,0:T(8,128)} %reshape.135, pred[128,256]{1,0:T(8,128)(4,1)S(1)} %fusion.16, bf16[128,16,128]{2,0,1:T(8,128)(2,1)} %copy.27, bf16[128,16,128]{2,0,1:T(8,128)(2,1)} %copy.26, f32[128,16,128]{0,2,1:T(8,128)S(1)} %bitcast.39, ...), kind=kOutput, calls=%fused_computation.4 | convolution fusion | flops 140511744 | bytes 8437760 | tf_op jit(solution)/shard_map/div | solution.py:57
  51.2 2.6 %fusion.4 = bf16[16,128,256]{2,1,0:T(8,128)(2,1)S(1)} fusion(f32[16,256,128]{1,2,0:T(8,128)} %fusion.6, f32[16,128,256]{2,1,0:T(8,128)} %get-tuple-element.23, f32[16,128]{1,0:T(8,128)S(1)} %get-tuple-element.22), kind=kLoop, calls=%fused_computation.6 | loop fusion | flops 2097152 | bytes 5251072 | tf_op jit(solution)/shard_map/convert_element_type | solution.py:61
  53.7 1.2 reshape.136
  54.9 2.5 %pad.13 = bf16[16,257,128]{2,1,0:T(8,128)(2,1)} pad(bf16[16,256,128]{2,1,0:T(8,128)(2,1)} %reshape.136, bf16[]{:T(256)} %constant.22.clone.1), padding=0_0x1_0x0_0 | pad | bytes 2101250 | tf_op jit(solution)/shard_map/transpose(jvp())/pad | solution.py:22
  57.4 5.0 %reshape.137 = bf16[16,128,257]{2,1,0:T(8,128)(2,1)} reshape(bf16[16,257,128]{2,1,0:T(8,128)(2,1)} %pad.13) | data formatting | bytes 2105344 | tf_op jit(solution)/shard_map/transpose(jvp())/reshape | solution.py:22
  62.5 3.6 %fusion.10 = f32[16,128,256]{2,1,0:T(8,128)} fusion(bf16[16,128,257]{2,1,0:T(8,128)(2,1)} %reshape.137, f32[128,16,128]{0,2,1:T(8,128)S(1)} %bitcast.40, f32[16,128]{1,0:T(8,128)S(1)} %bitcast.50), kind=kOutput, calls=%fused_computation.21 | convolution fusion | flops 134742016 | bytes 4202496 | tf_op jit(solution)/shard_map/hip,ihd->phd/dot_general | solution.py:16
  66.1 2.9 %copy.41 = f32[256,2048]{1,0:T(8,128)} copy(f32[256,2048]{0,1:T(8,128)} %bitcast.44) | data formatting | bytes 4194304 | tf_op jit(solution)/shard_map/reshape | solution.py:68
  68.9 0.0 reduce-scatter.3.cloned.1.call-update
  69.0 0.2 reduce-scatter.5.cloned.1.call-start
  69.2 31.7 %reduce-scatter.3.cloned.1.call-done = f32[64,2048]{1,0:T(8,128)} async-done(((f32[256,2048]{1,0:T(8,128)}), f32[64,2048]{1,0:T(8,128)}) %reduce-scatter.3.cloned.1.call-update) | async-done | bytes 524304 | tf_op jit(solution)/shard_map/reduce_scatter | solution.py:100
  100.8 0.0 reduce-scatter.5.cloned.1.call-update
  100.9 0.0 copy-start
  100.9 1.8 %convolution_bitcast_fusion.1 = f32[128,16,128]{0,2,1:T(8,128)S(1)} fusion(bf16[16,128,256]{2,1,0:T(8,128)(2,1)S(1)} %fusion.4, bf16[128,16,128]{2,0,1:T(8,128)(2,1)} %copy.27, bf16[128,16,128]{2,0,1:T(8,128)(2,1)} %copy.26), kind=kOutput, calls=%fused_computation.11 | convolution fusion | flops 136314880 | bytes 3145728 | tf_op jit(solution)/shard_map/hij,jhd->ihd/dot_general | solution.py:16
  102.7 0.0 copy-done
  102.7 1.4 fusion.21
  104.0 2.0 %copy.42 = bf16[1,128,2048]{2,1,0:T(8,128)(2,1)} copy(bf16[1,128,2048]{1,2,0:T(8,128)(2,1)} %bitcast.46) | data formatting | bytes 1048576
  106.1 0.5 convolution_convert_fusion
  106.5 1.0 copy.43
  107.6 10.5 %all-reduce.3 = (f32[2048]{0:T(1024)S(1)}, f32[2048]{0:T(1024)S(1)}) all-reduce(f32[2048]{0:T(1024)S(1)} %bitcast.52, f32[2048]{0:T(1024)S(1)} %bitcast.51), channel_id=1, replica_groups=mesh['seg'=4,'dp'=8] {'seg'}, use_global_device_ids=true, to_apply=%region_6.7 | all-reduce | flops 4096 | bytes 32768 | tf_op jit(solution)/shard_map/psum | solution.py:99
  118.1 37.4 %all-reduce.2 = (f32[2048]{0:T(1024)}, f32[2048]{0:T(1024)}) all-reduce(f32[2048]{0:T(1024)S(1)} %get-tuple-element.17, f32[2048]{0:T(1024)S(1)} %get-tuple-element.18), channel_id=1, replica_groups=mesh['seg'=4,'dp'=8] {'dp'}, use_global_device_ids=true, to_apply=%region_7.8 | all-reduce | flops 4096 | bytes 32768 | tf_op jit(solution)/shard_map/psum | solution.py:99
  155.5 12.1 %reduce-scatter.5.cloned.1.call-done = f32[64,256]{1,0:T(8,128)} async-done(((f32[64,2048]{1,0:T(8,128)}), f32[64,256]{1,0:T(8,128)}) %reduce-scatter.5.cloned.1.call-update) | async-done | bytes 65552 | tf_op jit(solution)/shard_map/reduce_scatter | solution.py:101
  (4 shorter events, 0.0 us)
Async XLA Ops:
  7.2 12.1 %copy-start.2 = (bf16[1,128,2048]{2,1,0:T(8,128)(2,1)S(1)}, bf16[1,128,2048]{2,1,0:T(8,128)(2,1)}, u32[]{:S(2)}) copy-start(bf16[1,128,2048]{2,1,0:T(8,128)(2,1)} %param.7) | copy-start | bytes 1572868
  7.2 12.3 %copy-start.1 = (bf16[256,2048]{1,0:T(8,128)(2,1)S(1)}, bf16[256,2048]{1,0:T(8,128)(2,1)}, u32[]{:S(2)}) copy-start(bf16[256,2048]{1,0:T(8,128)(2,1)} %param.10) | copy-start | bytes 3145732
  7.2 93.7 %reduce-scatter.3.cloned.1.call-start = ((), (), s32[]{:S(2)}) async-start(), calls=%async_computation.2 | async-start | bytes 2621440 | tf_op jit(solution)/shard_map/reduce_scatter | solution.py:100
  9.4 29.4 %collective-permute-start.1 = (bf16[128,2048]{0,1:T(8,128)(2,1)}, bf16[128,2048]{0,1:T(8,128)(2,1)}, u32[]{:S(2)}, u32[]{:S(2)}) collective-permute-start(bf16[128,2048]{0,1:T(8,128)(2,1)} %bitcast.5), channel_id=1, source_target_pairs={{0,8},{8,16},{16,24},{1,9},{9,17},{17,25},{2,10},{10,18},{18,26},{... | collective-permute-start | bytes 1572872 | tf_op jit(solution)/shard_map/ppermute | solution.py:12
  14.6 5.4 %copy-start.3 = (f32[2048]{0:T(1024)S(1)}, f32[2048]{0:T(1024)}, u32[]{:S(2)}) copy-start(f32[2048]{0:T(1024)} %param.12) | copy-start | bytes 24580
  14.6 26.3 %collective-permute-start = (bf16[128,2048]{0,1:T(8,128)(2,1)}, bf16[128,2048]{0,1:T(8,128)(2,1)}, u32[]{:S(2)}, u32[]{:S(2)}) collective-permute-start(bf16[128,2048]{0,1:T(8,128)(2,1)} %bitcast), channel_id=1, source_target_pairs={{0,8},{8,16},{16,24},{1,9},{9,17},{17,25},{2,10},{10,18},{18,26},{... | collective-permute-start | bytes 1572872 | tf_op jit(solution)/shard_map/ppermute | solution.py:12
  42.9 2.8 %copy-start.4 = (f32[2048]{0:T(1024)S(1)}, f32[2048]{0:T(1024)}, u32[]{:S(2)}) copy-start(f32[2048]{0:T(1024)} %param.11) | copy-start | bytes 24580
  69.0 98.6 %reduce-scatter.5.cloned.1.call-start = ((), (), s32[]{:S(2)}) async-start(), calls=%async_computation.3 | async-start | bytes 589824 | tf_op jit(solution)/shard_map/reduce_scatter | solution.py:101
  100.9 1.8 %copy-start = (bf16[16,128,257]{2,1,0:T(8,128)(2,1)S(1)}, bf16[16,128,257]{2,1,0:T(8,128)(2,1)}, u32[]{:S(2)}) copy-start(bf16[16,128,257]{2,1,0:T(8,128)(2,1)} %reshape.137) | copy-start | bytes 3158020
Sparse Core Ops, SparseCore 0:
  69.1 31.7 reduce-scatter.2
  105.1 62.3 reduce-scatter.4
